TPU v7x, 32 devices: a whole 2x2x4 slice. The times are simulated.
32 devices in a mesh: dp: 8 (over z, x), tensor: 4 (over y, core).
Axes of the slice: x: 2, y: 2, z: 4, core: 2. Of those that a mesh axis runs over, the one named last changes fastest.
Arguments:
- attn_out: bfloat16 [4096, 8192], P('dp', 'tensor'), may hold values from -6 to 6
- frozen_weight: bfloat16 [8192, 8192], P('tensor', 'dp'), may hold values from -0.0625 to 0.0625
- vector_bank: float32 [256, 256], replicated, may hold values from -0.18 to 0.18
- logits_a: float32 [16, 32, 2], P(None, 'tensor'), may hold values from -2 to 2
- index_a: int32 [16, 32, 2], P(None, 'tensor'), may hold values from 0 to 255, all different within a row
- logits_b: float32 [16, 32, 2], P(None, 'tensor'), may hold values from -2 to 2
- index_b: int32 [16, 32, 2], P(None, 'tensor'), may hold values from 0 to 255, all different within a row
- out_grad: bfloat16 [4096, 8192], P('dp'), may hold values from -6 to 6
Outputs:
- layer_out: bfloat16 [4096, 8192], P('dp', 'tensor')
- attn_grad: bfloat16 [4096, 8192], P('dp', 'tensor')
- bank_grad: float32 [256, 256], replicated
- logits_a_grad: float32 [16, 32, 2], P(None, 'tensor')
- logits_b_grad: float32 [16, 32, 2], P(None, 'tensor')
Inputs may be any that keep to these rules, and one draw needn't show every extreme that they name: `index_a`: the 2 entries of one sub-vector differ. `index_b`: the 2 entries of one sub-vector differ.
All inputs are finite; a program needn't handle non-finite values.
Results may differ from a plain program's by a relative error of at most 0.014.
Values may be sent and summed in bfloat16 or wider, within the bound.
A program may use at most 128 MiB of HBM per device.

v0:
```python
import jax
import jax.numpy as jnp
from jax import lax
from jax.sharding import PartitionSpec as P

adapter_scale = 2.0


def compose(logits, indices, vector_bank):
    weights = jax.nn.sigmoid(logits - logits[..., ::-1])
    levels = jnp.arange(vector_bank.shape[0], dtype=jnp.int32)
    picked = (indices[..., None] == levels).astype(jnp.float32)
    mixing = jnp.sum(picked * weights[..., None], axis=2)
    blocks = jnp.einsum("rjb,bc->rjc", mixing, vector_bank, precision=lax.Precision.HIGHEST)
    return (weights, picked, mixing, blocks.reshape(blocks.shape[0], -1))


def compose_back(grad_rows, weights, picked, mixing, vector_bank):
    blocks = grad_rows.reshape(mixing.shape[0], mixing.shape[1], -1)
    bank_part = jnp.einsum("rjb,rjc->bc", mixing, blocks, precision=lax.Precision.HIGHEST)
    projected = jnp.einsum("rjc,bc->rjb", blocks, vector_bank, precision=lax.Precision.HIGHEST)
    dots = jnp.sum(picked * projected[:, :, None, :], axis=3)
    logit_grad = weights * (dots - jnp.sum(weights * dots, axis=2, keepdims=True))
    return (bank_part, logit_grad)


def local(attn_out, frozen_weight, vector_bank, logits_a, index_a, logits_b, index_b, out_grad):
    weights_a, picked_a, mixing_a, rows_a = compose(logits_a, index_a, vector_bank)
    weights_b, picked_b, mixing_b, rows_b = compose(logits_b, index_b, vector_bank)
    down_a = rows_a.astype(jnp.bfloat16)
    up_b = rows_b.astype(jnp.bfloat16)
    own_width = up_b.shape[1]
    grad_cols = lax.dynamic_slice_in_dim(
        out_grad, lax.axis_index("tensor") * own_width, own_width, 1
    )
    low_part = jnp.dot(attn_out, down_a.T, preferred_element_type=jnp.float32)
    back_part = jnp.dot(grad_cols, up_b.T, preferred_element_type=jnp.float32)
    low_total = lax.psum(low_part, "tensor")
    low_bf = low_total.astype(jnp.bfloat16)
    gathered = lax.all_gather(frozen_weight, "dp", axis=1, tiled=True)
    partial_value = jnp.dot(attn_out, gathered, preferred_element_type=jnp.float32).astype(
        jnp.bfloat16
    )
    summed = lax.psum_scatter(partial_value, "tensor", scatter_dimension=1, tiled=True).astype(
        jnp.float32
    )
    layer_out = (
        summed + adapter_scale * jnp.dot(low_bf, up_b, preferred_element_type=jnp.float32)
    ).astype(jnp.bfloat16)
    back_total = lax.psum(back_part, "tensor")
    back_bf = back_total.astype(jnp.bfloat16)
    main = lax.dot_general(
        out_grad, gathered, (((1,), (1,)), ((), ())), preferred_element_type=jnp.float32
    )
    attn_grad = (
        main + adapter_scale * jnp.dot(back_bf, down_a, preferred_element_type=jnp.float32)
    ).astype(jnp.bfloat16)
    factor = adapter_scale / (attn_out.shape[0] * lax.axis_size("dp"))
    grad_a = factor * lax.dot_general(
        back_bf, attn_out, (((0,), (0,)), ((), ())), preferred_element_type=jnp.float32
    )
    grad_b = factor * lax.dot_general(
        low_bf, grad_cols, (((0,), (0,)), ((), ())), preferred_element_type=jnp.float32
    )
    bank_a, logit_grad_a = compose_back(grad_a, weights_a, picked_a, mixing_a, vector_bank)
    bank_b, logit_grad_b = compose_back(grad_b, weights_b, picked_b, mixing_b, vector_bank)
    bank_part = bank_a + bank_b
    bank_group = lax.psum(bank_part, "tensor")
    bank_grad, logits_a_grad, logits_b_grad = lax.psum(
        (bank_group, logit_grad_a, logit_grad_b), "dp"
    )
    return (layer_out, attn_grad, bank_grad, logits_a_grad, logits_b_grad)


def solution(mesh):
    return jax.shard_map(
        local,
        mesh=mesh,
        in_specs=(
            P("dp", "tensor"),
            P("tensor", "dp"),
            P(),
            P(None, "tensor", None),
            P(None, "tensor", None),
            P(None, "tensor", None),
            P(None, "tensor", None),
            P("dp", None),
        ),
        out_specs=(
            P("dp", "tensor"),
            P("dp", "tensor"),
            P(),
            P(None, "tensor", None),
            P(None, "tensor", None),
        ),
        check_vma=False,
    )
```

profile of v0, /device:TPU:0, one launch (start us, length us, event | category | flops | bytes accessed | tf_op | source)
XLA Modules:
  0.0 792.0 jit_solution(11416128303065305518)
XLA Ops:
  8.1 0.7 all-gather.2.cloned.1.call-update
  8.9 0.1 copy.36
  9.0 0.1 copy.33
  9.1 0.1 select_reduce_fusion.3
  9.2 0.3 convolution_convert_fusion.2
  9.5 0.2 copy-done
  9.7 0.6 convolution_bitcast_fusion.2
  10.4 12.9 %psum.42 = bf16[512,16]{0,1:T(8,128)(2,1)S(1)} all-reduce(f32[512,16]{0,1:T(8,128)S(1)} %convolution_bitcast_fusion.2), channel_id=1, replica_groups=mesh['dp'=8,'tensor'=4] {'tensor'}, use_global_device_ids=true, to_apply=%region_2.0 | all-reduce | flops 8192 | bytes 49152 | tf_op jit(solution)/shard_map/psum | solution.py:38
  23.3 2.1 convolution_multiply_fusion
  25.5 0.1 copy.37
  25.6 0.1 copy.40
  25.7 0.4 fusion.4
  26.1 0.2 select_reduce_fusion
  26.3 0.3 convolution_convert_fusion.1
  26.6 2.2 fusion.1
  28.9 11.5 %psum.43 = bf16[512,16]{0,1:T(8,128)(2,1)S(1)} all-reduce(f32[512,16]{0,1:T(8,128)S(1)} %fusion.1), channel_id=1, replica_groups=mesh['dp'=8,'tensor'=4] {'tensor'}, use_global_device_ids=true, to_apply=%region_4.0 | all-reduce | flops 8192 | bytes 49152 | tf_op jit(solution)/shard_map/psum | solution.py:50
  40.3 0.4 convolution_multiply_fusion.1
  40.8 0.4 convolution_bitcast_fusion
  41.2 1.1 fusion.3
  42.4 608.5 %all-gather.2.cloned.1.call-done = bf16[2048,8192]{1,0:T(8,128)(2,1)} async-done(((bf16[2048,1024]{1,0:T(8,128)(2,1)}), bf16[2048,8192]{1,0:T(8,128)(2,1)}) %all-gather.2.cloned.1.call-update) | async-done | bytes 33554448 | tf_op jit(solution)/shard_map/all_gather | solution.py:40
  650.8 25.3 %convolution_convert_fusion = bf16[512,8192]{1,0:T(8,128)(2,1)} fusion(bf16[512,2048]{1,0:T(8,128)(2,1)S(1)} %copy-done, bf16[2048,8192]{1,0:T(8,128)(2,1)} %all-gather.2.cloned.1.call-done), kind=kOutput, calls=%fused_computation | convolution fusion | flops 17184063488 | bytes 44040192 | tf_op jit(solution)/shard_map/dot_general | solution.py:41
  676.3 0.4 fusion.6
  676.7 0.2 select_reduce_fusion.1
  677.1 36.0 %all-reduce = (f32[16,8,2]{0,1,2:T(8,128)S(1)}, f32[16,8,2]{0,1,2:T(8,128)S(1)}) all-reduce(f32[16,8,2]{0,1,2:T(8,128)S(1)} %get-tuple-element.20, f32[16,8,2]{0,1,2:T(8,128)S(1)} %get-tuple-element.19), channel_id=1, replica_groups=mesh['dp'=8,'tensor'=4] {'dp'}, use_global_device_ids=true, to_apply=%region_9.0 | all-reduce | flops 512 | bytes 4096 | tf_op jit(solution)/shard_map/psum | solution.py:69
  713.1 0.6 copy.45
  713.7 0.6 copy.46
  714.3 24.3 %fusion.24 = f32[512,2048]{1,0:T(8,128)S(1)} fusion(bf16[512,8192]{1,0:T(8,128)(2,1)} %param.15, bf16[2048,8192]{1,0:T(8,128)(2,1)} %all-gather.2.cloned.1.call-done), kind=kOutput, calls=%fused_computation.46 | convolution fusion | flops 17179869184 | bytes 46137344 | tf_op jit(solution)/shard_map/dot_general | solution.py:52
  738.6 2.0 add_convert_fusion
  740.7 6.7 reduce-scatter.2.cloned.1.call-done
  747.4 3.6 add_convert_fusion.1
  751.1 31.9 %all-reduce.6.cloned.1.call-done = f32[256,256]{1,0:T(8,128)} async-done(((f32[256,256]{1,0:T(8,128)}), f32[256,256]{1,0:T(8,128)}) %all-reduce.6.cloned.1.call-update) | async-done | bytes 262160 | tf_op jit(solution)/shard_map/psum | solution.py:69
  782.9 1.7 copy.53
  (34 shorter events, 0.6 us)
Async XLA Ops:
  8.0 1.7 copy-start
  8.0 0.8 copy-start.5
  8.0 0.9 copy-start.3
  8.0 1.2 copy-start.2
  8.0 17.4 %copy-start.4 = (s32[16,8,2]{0,2,1:T(2,128)S(1)}, s32[16,8,2]{0,2,1:T(2,128)}, u32[]{:S(2)}) copy-start(s32[16,8,2]{0,2,1:T(2,128)} %param.14) | copy-start | bytes 3076
  8.1 17.5 %copy-start.6 = (f32[16,8,2]{0,2,1:T(2,128)S(1)}, f32[16,8,2]{0,2,1:T(2,128)}, u32[]{:S(2)}) copy-start(f32[16,8,2]{0,2,1:T(2,128)} %param.13) | copy-start | bytes 3076
  8.1 642.8 %all-gather.2.cloned.1.call-start = ((), (), s32[]{:S(2)}) async-start(), calls=%async_computation.1 | async-start | bytes 37748736 | tf_op jit(solution)/shard_map/all_gather | solution.py:40
  8.8 705.5 %all-reduce.4.cloned.1.call-start = ((), (), s32[]{:S(2)}) async-start(), calls=%async_computation.3 | async-start | bytes 524288 | tf_op jit(solution)/shard_map/psum | solution.py:68
  42.3 705.1 %reduce-scatter.2.cloned.1.call-start = ((), (), s32[]{:S(2)}) async-start(), calls=%async_computation.2 | async-start | bytes 10485760 | tf_op jit(solution)/shard_map/reduce_scatter | solution.py:44
  676.2 106.7 %all-reduce.6.cloned.1.call-start = ((), (), s32[]{:S(2)}) async-start(), calls=%async_computation.4 | async-start | bytes 524288 | tf_op jit(solution)/shard_map/psum | solution.py:69
  714.3 70.3 %copy-start.1 = (bf16[512,2048]{1,0:T(8,128)(2,1)S(1)}, bf16[512,2048]{1,0:T(8,128)(2,1)}, u32[]{:S(2)}) copy-start(bf16[512,2048]{1,0:T(8,128)(2,1)} %param.8) | copy-start | bytes 6291460
Sparse Core Ops, SparseCore 0:
  10.4 640.3 all-gather.1
  714.4 68.4 all-reduce.5
Sparse Core Ops, SparseCore 1:
  42.4 32.2 all-reduce.3
  676.3 71.1 reduce-scatter.1
where the time goes:
time: 792 us
  waiting for transfers between devices  648 us (82%)
  matrix products  63.7 us (8%)
  blocking collectives  60.4 us (8%)
  between operations  15.7 us (2%)
    all_gather x1, waiting for transfers between devices, local(): gathered = lax.all_gather(frozen_weight, 'dp', axis=1, tiled=True)  608 us
    psum x1, blocking collectives, local(): lax.psum((bank_group, logit_grad_a, logit_grad_b), 'dp')  36 us
    psum x1, waiting for transfers between devices, local(): lax.psum((bank_group, logit_grad_a, logit_grad_b), 'dp')  31.9 us
    dot_general x1, matrix products, local(): jnp.dot(attn_out, gathered, preferred_element_type=jnp.float32)  25.3 us
    dot_general x1, matrix products, local(): lax.dot_general(out_grad, gathered, (((1,), (1,)), ((), ())), preferred_e...  24.3 us
  transfers between devices with their start and end apart: 4, of which 3 were waited for; matrix products, arithmetic and copies ran while one was open for 8% of the time, Pallas kernels for 0%

commit v1 on v0

--- a/solution.py
+++ b/solution.py
@@ -37,7 +37,7 @@
     back_part = jnp.dot(grad_cols, up_b.T, preferred_element_type=jnp.float32)
     low_total = lax.psum(low_part, "tensor")
     low_bf = low_total.astype(jnp.bfloat16)
-    gathered = lax.all_gather(frozen_weight, "dp", axis=1, tiled=True)
+    gathered = jnp.concatenate(lax.all_gather(frozen_weight, "dp"), axis=1)
     partial_value = jnp.dot(attn_out, gathered, preferred_element_type=jnp.float32).astype(
         jnp.bfloat16
     )

time: 792 us -> 835 us (1.054)
  local copies, waits for them, and re-layouts: 3.69 us -> 45.9 us
    reshape x0 -> x1, local copies, waits for them, and re-layouts: none -> 42.2 us  [local(): gathered = jnp.concatenate(lax.all_gather(frozen_weight, 'dp'), axis=1)]
  transfers between devices with their start and end apart: 4 -> 4, of which waited for: 3 -> 3; matrix products, arithmetic and copies ran while one was open for 8% -> 13% of each run, Pallas kernels for 0% -> 0%
where the time goes in v1:
time: 835 us; the launch traced here: 833 us
  waiting for transfers between devices  648 us (78%)
  matrix products  62.5 us (7%)
  blocking collectives  60.3 us (7%)
  local copies, waits for them, and re-layouts  45.9 us (5%)
  between operations  15.7 us (2%)
    all_gather x1, waiting for transfers between devices, local(): gathered = jnp.concatenate(lax.all_gather(frozen_weight, 'dp'), axis=1)  608 us
    reshape x1, local copies, waits for them, and re-layouts, local(): gathered = jnp.concatenate(lax.all_gather(frozen_weight, 'dp'), axis=1)  42.2 us
    psum x1, blocking collectives, local(): lax.psum((bank_group, logit_grad_a, logit_grad_b), 'dp')  35.9 us
    psum x1, waiting for transfers between devices, local(): lax.psum((bank_group, logit_grad_a, logit_grad_b), 'dp')  31.9 us
    dot_general x1, matrix products, local(): jnp.dot(attn_out, gathered, preferred_element_type=jnp.float32)  24.3 us
    dot_general x1, matrix products, local(): lax.dot_general(out_grad, gathered, (((1,), (1,)), ((), ())), preferred_e...  24.2 us
  transfers between devices with their start and end apart: 4, of which 3 were waited for; matrix products, arithmetic and copies ran while one was open for 13% of the time, Pallas kernels for 0%

profile of v1, /device:TPU:0, one launch (start us, length us, event | category | flops | bytes accessed | tf_op | source)
XLA Modules:
  0.0 833.2 jit_solution(2812677365234545207)
XLA Ops:
  8.1 0.7 all-gather.3.cloned.1.call-update
  8.9 0.1 copy.55
  9.0 0.1 copy.52
  9.1 0.1 select_reduce_fusion.3
  9.2 0.3 convolution_convert_fusion.2
  9.5 0.2 copy-done
  9.7 0.6 convolution_bitcast_fusion.2
  10.4 12.9 %psum.42 = bf16[512,16]{0,1:T(8,128)(2,1)S(1)} all-reduce(f32[512,16]{0,1:T(8,128)S(1)} %convolution_bitcast_fusion.2), channel_id=1, replica_groups=mesh['dp'=8,'tensor'=4] {'tensor'}, use_global_device_ids=true, to_apply=%region_2.0 | all-reduce | flops 8192 | bytes 49152 | tf_op jit(solution)/shard_map/psum | solution.py:38
  23.3 2.1 convolution_multiply_fusion
  25.5 0.1 copy.56
  25.7 0.4 fusion.4
  26.1 0.2 select_reduce_fusion
  26.3 0.3 convolution_convert_fusion.1
  26.6 2.2 fusion.1
  28.9 11.5 %psum.43 = bf16[512,16]{0,1:T(8,128)(2,1)S(1)} all-reduce(f32[512,16]{0,1:T(8,128)S(1)} %fusion.1), channel_id=1, replica_groups=mesh['dp'=8,'tensor'=4] {'tensor'}, use_global_device_ids=true, to_apply=%region_4.0 | all-reduce | flops 8192 | bytes 49152 | tf_op jit(solution)/shard_map/psum | solution.py:50
  40.3 0.4 convolution_multiply_fusion.1
  40.8 0.4 convolution_bitcast_fusion
  41.2 1.1 fusion.3
  42.4 608.4 %all-gather.3.cloned.1.call-done = bf16[16384,1024]{1,0:T(8,128)(2,1)} async-done(((bf16[2048,1024]{1,0:T(8,128)(2,1)}), bf16[16384,1024]{1,0:T(8,128)(2,1)}) %all-gather.3.cloned.1.call-update) | async-done | bytes 33554448 | tf_op jit(solution)/shard_map/all_gather | solution.py:40
  650.8 42.2 %copy.51 = bf16[2048,8,1024]{0,2,1:T(8,128)(2,1)} copy(bf16[2048,8,1024]{2,0,1:T(8,128)(2,1)} %bitcast.51) | data formatting | bytes 67108864 | tf_op jit(solution)/shard_map/reshape | solution.py:40
  693.1 24.3 %convolution_convert_fusion = bf16[512,8192]{1,0:T(8,128)(2,1)} fusion(bf16[512,2048]{1,0:T(8,128)(2,1)S(1)} %copy-done, bf16[2048,8192]{0,1:T(8,128)(2,1)} %bitcast.52), kind=kOutput, calls=%fused_computation | convolution fusion | flops 17184063488 | bytes 44040192 | tf_op jit(solution)/shard_map/dot_general | solution.py:41
  717.5 0.4 fusion.6
  717.9 0.2 select_reduce_fusion.1
  718.3 35.9 %all-reduce = (f32[16,8,2]{0,1,2:T(8,128)S(1)}, f32[16,8,2]{0,1,2:T(8,128)S(1)}) all-reduce(f32[16,8,2]{0,1,2:T(8,128)S(1)} %get-tuple-element.20, f32[16,8,2]{0,1,2:T(8,128)S(1)} %get-tuple-element.19), channel_id=1, replica_groups=mesh['dp'=8,'tensor'=4] {'dp'}, use_global_device_ids=true, to_apply=%region_9.0 | all-reduce | flops 512 | bytes 4096 | tf_op jit(solution)/shard_map/psum | solution.py:69
  754.2 0.6 copy.64
  754.8 0.6 copy.65
  755.4 24.2 %fusion.24 = f32[512,2048]{1,0:T(8,128)S(1)} fusion(bf16[512,8192]{1,0:T(8,128)(2,1)} %param.15, bf16[2048,8192]{0,1:T(8,128)(2,1)} %bitcast.53), kind=kOutput, calls=%fused_computation.46 | convolution fusion | flops 17179869184 | bytes 46137344 | tf_op jit(solution)/shard_map/dot_general | solution.py:52
  779.7 2.0 add_convert_fusion
  781.7 6.9 reduce-scatter.2.cloned.1.call-done
  788.6 3.6 add_convert_fusion.1
  792.2 31.9 %all-reduce.6.cloned.1.call-done = f32[256,256]{1,0:T(8,128)} async-done(((f32[256,256]{1,0:T(8,128)}), f32[256,256]{1,0:T(8,128)}) %all-reduce.6.cloned.1.call-update) | async-done | bytes 262160 | tf_op jit(solution)/shard_map/psum | solution.py:69
  824.1 1.7 copy.72
  (35 shorter events, 0.7 us)
Async XLA Ops:
  8.0 1.7 copy-start
  8.0 0.8 copy-start.5
  8.0 0.9 copy-start.3
  8.0 1.2 copy-start.2
  8.0 17.4 %copy-start.4 = (s32[16,8,2]{0,2,1:T(2,128)S(1)}, s32[16,8,2]{0,2,1:T(2,128)}, u32[]{:S(2)}) copy-start(s32[16,8,2]{0,2,1:T(2,128)} %param.14) | copy-start | bytes 3076
  8.1 17.5 %copy-start.6 = (f32[16,8,2]{0,2,1:T(2,128)S(1)}, f32[16,8,2]{0,2,1:T(2,128)}, u32[]{:S(2)}) copy-start(f32[16,8,2]{0,2,1:T(2,128)} %param.13) | copy-start | bytes 3076
  8.1 642.8 %all-gather.3.cloned.1.call-start = ((), (), s32[]{:S(2)}) async-start(), calls=%async_computation.4 | async-start | bytes 37748736 | tf_op jit(solution)/shard_map/all_gather | solution.py:40
  8.8 746.6 %all-reduce.4.cloned.1.call-start = ((), (), s32[]{:S(2)}) async-start(), calls=%async_computation.2 | async-start | bytes 524288 | tf_op jit(solution)/shard_map/psum | solution.py:68
  42.3 746.3 %reduce-scatter.2.cloned.1.call-start = ((), (), s32[]{:S(2)}) async-start(), calls=%async_computation.1 | async-start | bytes 10485760 | tf_op jit(solution)/shard_map/reduce_scatter | solution.py:44
  717.4 106.7 %all-reduce.6.cloned.1.call-start = ((), (), s32[]{:S(2)}) async-start(), calls=%async_computation.3 | async-start | bytes 524288 | tf_op jit(solution)/shard_map/psum | solution.py:69
  755.4 70.3 %copy-start.1 = (bf16[512,2048]{1,0:T(8,128)(2,1)S(1)}, bf16[512,2048]{1,0:T(8,128)(2,1)}, u32[]{:S(2)}) copy-start(bf16[512,2048]{1,0:T(8,128)(2,1)} %param.8) | copy-start | bytes 6291460
Sparse Core Ops, SparseCore 0:
  10.4 640.3 all-gather.2
  755.6 68.5 all-reduce.5
Sparse Core Ops, SparseCore 1:
  42.4 32.2 all-reduce.3
  717.5 71.1 reduce-scatter.1
